TPU v7x, 128 devices: a whole 4x4x4 slice. The times are simulated.
128 devices in a mesh: lon: 8 (over x_hi, y), lat: 8 (over z, core), batch: 2 (over x_lo).
Axes of the slice: x: 4 (x_hi: 2, x_lo: 2; x = x_hi * 2 + x_lo), y: 4, z: 4, core: 2. Of those that a mesh axis runs over, the one named last changes fastest.
Arguments:
- state: bfloat16 [2, 21, 256, 4096], P('batch', None, 'lat', 'lon'), may hold values from -6 to 6
- forcing: bfloat16 [2, 96, 256, 4096], P('batch', None, 'lat', 'lon'), may hold values from -6 to 6
- land_mask: int32 [256, 4096], P('lat', 'lon'), may hold values 0 or 1
- partner: int32 [4096], P('lon'), may hold values from 0 to 4095, as said below
- cotangent: bfloat16 [2, 512, 128, 2048], P('batch', None, 'lat', 'lon'), may hold values from -6 to 6
- weight_state: bfloat16 [512, 336], replicated, may hold values from -0.125 to 0.125
- weight_force: bfloat16 [512, 1536], replicated, may hold values from -0.125 to 0.125
Outputs:
- grad_state: bfloat16 [2, 21, 256, 4096], P('batch', None, 'lat', 'lon')
- grad_forcing: bfloat16 [2, 96, 256, 4096], P('batch', None, 'lat', 'lon')
- grad_wstate: float32 [512, 336], P(('lat', 'batch'))
- grad_wforce: float32 [512, 1536], P(('lat', 'batch'))
Inputs may be any that keep to these rules, and one draw needn't show every extreme that they name: partner is an involution that maps the columns of the k-th block of 512 columns onto the columns of the block k-th from the other end, in an order drawn for each pair of blocks.
All inputs are finite; a program needn't handle non-finite values. No bound on the sum of `land_mask` on one device may be relied on, other than what follows from the above.
Results may differ from a plain program's by a relative error of at most 0.0011.
Values may be sent and summed in bfloat16 or wider, within the bound.
A program may use at most 256 MiB of HBM per device.

v0:
```python
import math
import jax
import jax.numpy as jnp
from jax import lax
from jax.sharding import PartitionSpec as P


def partner_2(block, axis, distance):
    count = lax.axis_size(axis)
    route = []
    for low in range(count):
        high = low | 1 << distance
        if high != low and high < count:
            route += [(low, high), (high, low)]
    return lax.ppermute(block, axis, route)


def with_halo(cells, sides, width):
    for axis, dim in sides:
        count = lax.axis_size(axis)
        head = lax.slice_in_dim(cells, 0, width, axis=dim)
        tail = lax.slice_in_dim(cells, cells.shape[dim] - width, cells.shape[dim], axis=dim)
        cells = jnp.concatenate(
            [
                lax.ppermute(tail, axis, [(i, (i + 1) % count) for i in range(count)]),
                cells,
                lax.ppermute(head, axis, [((i + 1) % count, i) for i in range(count)]),
            ],
            axis=dim,
        )
    return cells


def on_device(state, forcing, land_mask, partner, cotangent, weight_state, weight_force):
    state_ch = state.shape[1]
    channels = state_ch + forcing.shape[1]
    cell_rows = state.shape[2]
    cell_cols = state.shape[3]
    feat_width = cotangent.shape[1]
    tok_rows = cell_rows // 2
    tok_cols = cell_cols // 2
    lon_count = lax.axis_size("lon")
    lat_count = lax.axis_size("lat")
    batch_count = lax.axis_size("batch")
    lon_at = lax.axis_index("lon")
    lat_at = lax.axis_index("lat")
    at_top = lat_at == lat_count - 1
    at_bottom = lat_at == 0
    mirror_base = (lon_count - 1 - lon_at) * cell_cols
    local_col = partner - mirror_base
    bit_count = lon_count.bit_length() - 1
    bit_order = list(range(bit_count))
    masked = jnp.concatenate([state[0], forcing[0]], axis=0) * land_mask.astype(jnp.bfloat16)
    paired = masked[:, cell_rows - 1, :]
    for bit_pos in bit_order:
        paired = partner_2(paired, "lon", bit_pos)
    fold_row = jnp.take(paired, local_col, axis=1)
    row_ext = with_halo(masked, (("lat", 1),), 1)
    south_row = jnp.where(at_bottom, jnp.zeros_like(row_ext[:, 0, :]), row_ext[:, 0, :])
    north_row = jnp.where(at_top, fold_row, row_ext[:, cell_rows + 1, :])
    row_ext = jnp.concatenate(
        [south_row[:, None, :], row_ext[:, 1 : cell_rows + 1, :], north_row[:, None, :]], axis=1
    )
    padded = with_halo(row_ext, (("lon", 2),), 1)
    planes = [[padded[:, row_par::2, col_par::2] for col_par in range(2)] for row_par in range(2)]
    windows = []
    for row_off in range(4):
        for col_off in range(4):
            plane = planes[row_off % 2][col_off % 2]
            row_start = row_off // 2
            col_start = col_off // 2
            windows.append(
                plane[:, row_start : row_start + tok_rows, col_start : col_start + tok_cols]
            )
    grad_tokens = cotangent[0]
    scale = 1.0 / math.sqrt(
        cotangent.shape[0] * batch_count * tok_rows * lat_count * tok_cols * lon_count
    )
    share = feat_width // (lat_count * batch_count)
    terms = [
        lax.dot_general(
            grad_tokens, window, (((1, 2), (1, 2)), ((), ())), preferred_element_type=jnp.float32
        )
        for window in windows
    ]
    summed = lax.psum(
        jnp.stack(terms, axis=-1).reshape(grad_tokens.shape[0], channels * 16) * scale,
        ("lon", "lat", "batch"),
    )
    kernel_own = lax.dynamic_slice_in_dim(
        summed, lax.axis_index(("lat", "batch")) * share, share, 0
    )
    grad_ext = with_halo(cotangent[0], (("lat", 1), ("lon", 2)), 1)
    south_tok = jnp.where(at_bottom, jnp.zeros_like(grad_ext[:, :1, :]), grad_ext[:, :1, :])
    north_tok = jnp.where(at_top, jnp.zeros_like(grad_ext[:, -1:, :]), grad_ext[:, -1:, :])
    grad_ext = jnp.concatenate([south_tok, grad_ext[:, 1 : tok_rows + 1, :], north_tok], axis=1)
    weights = jnp.concatenate([weight_state, weight_force], axis=1)
    spread_all = lax.dot_general(
        weights, grad_ext, (((0,), (0,)), ((), ())), preferred_element_type=jnp.float32
    )
    spread_all = spread_all.reshape(channels, 4, 4, tok_rows + 2, tok_cols + 2)
    parity_terms = (((1, 1), (3, 0)), ((0, 2), (2, 1)))
    fold_cols = []
    for col_par in range(2):
        acc_fold = jnp.zeros((channels, tok_cols), jnp.float32)
        for col_off, col_start in parity_terms[col_par]:
            acc_fold = (
                acc_fold + spread_all[:, 3, col_off, tok_rows, col_start : col_start + tok_cols]
            )
        fold_cols.append(acc_fold)
    fold_part = jnp.stack(fold_cols, axis=-1).reshape(channels, cell_cols)
    arrived = jnp.zeros((channels, cell_cols), jnp.float32).at[:, local_col].set(fold_part)
    for bit_pos in bit_order:
        arrived = partner_2(arrived.astype(jnp.bfloat16), "lon", bit_pos).astype(arrived.dtype)
    arrived = jnp.where(at_top, arrived, jnp.zeros_like(arrived))
    mask_float = land_mask.astype(jnp.float32)
    row_blocks = []
    for row_par in range(2):
        col_blocks = []
        for col_par in range(2):
            acc_cells = jnp.zeros((channels, tok_rows, tok_cols), jnp.float32)
            for row_off, row_start in parity_terms[row_par]:
                for col_off, col_start in parity_terms[col_par]:
                    acc_cells = (
                        acc_cells
                        + spread_all[
                            :,
                            row_off,
                            col_off,
                            row_start : row_start + tok_rows,
                            col_start : col_start + tok_cols,
                        ]
                    )
            if row_par == 1:
                acc_cells = acc_cells.at[:, tok_rows - 1, :].add(arrived[:, col_par::2])
            mask_plane = mask_float[row_par::2, col_par::2]
            col_blocks.append((acc_cells * mask_plane).astype(jnp.bfloat16))
        row_blocks.append(jnp.stack(col_blocks, axis=-1))
    result = jnp.stack(row_blocks, axis=2).reshape(channels, cell_rows, cell_cols)
    return (
        result[None, :state_ch],
        result[None, state_ch:],
        kernel_own[:, : state_ch * 16],
        kernel_own[:, state_ch * 16 :],
    )


def solution(mesh):
    in_specs = (
        P("batch", None, "lat", "lon"),
        P("batch", None, "lat", "lon"),
        P("lat", "lon"),
        P("lon"),
        P("batch", None, "lat", "lon"),
        P(),
        P(),
    )
    out_specs = (
        P("batch", None, "lat", "lon"),
        P("batch", None, "lat", "lon"),
        P(("lat", "batch"), None),
        P(("lat", "batch"), None),
    )
    return jax.shard_map(
        on_device, mesh=mesh, in_specs=in_specs, out_specs=out_specs, check_vma=False
    )
```

profile of v0, /device:TPU:1, one launch (start us, length us, event | category | flops | bytes accessed | tf_op | source)
XLA Modules:
  0.0 742.1 jit_solution(12922439610931023367)
XLA Ops:
  7.2 7.8 %copy.200 = bf16[1,512,16,256]{1,3,2,0:T(8,128)(2,1)} copy(bf16[1,512,16,256]{3,2,1,0:T(8,128)(2,1)} %param.15) | data formatting | bytes 8388608 | tf_op args[4]
  15.0 1.9 fusion.37
  18.3 1.6 collective-permute-start
  19.9 1.8 copy.317
  22.1 2.2 maximum_multiply_fusion
  24.3 1.9 copy-done.3
  26.9 2.0 collective-permute-start.11
  33.9 1.6 copy.199
  35.5 7.6 %copy.251 = bf16[512,16,256]{0,2,1:T(8,128)(2,1)} copy(bf16[512,16,256]{2,1,0:T(8,128)(2,1)} %bitcast.187) | data formatting | bytes 8388608 | tf_op jit(solution)/shard_map/squeeze | solution.py:93
  43.0 2.6 collective-permute-start.9
  46.7 2.8 collective-permute-start.3
  49.5 1.8 collective-permute-start.10
  51.4 4.5 collective-permute-done.2
  55.9 6.6 pad_maximum_fusion.1
  62.8 1.8 maximum_select_fusion.1
  64.6 22.9 %fusion = f32[1872,18,258]{2,0,1:T(8,128)} fusion(bf16[512,1,258]{0,2,1:T(8,128)(2,1)} %get-tuple-element.65, bf16[512,16,258]{0,2,1:T(8,128)(2,1)S(1)} %slice.297, bf16[512,1,258]{0,2,1:T(8,128)(2,1)S(1)} %get-tuple-element.64, bf16[512,1536]{0,1:T(8,128)(2,1)} %copy.199, bf16[512,336]{0,1:T(8,128)(2,1)} %param.16), kind=kOutput, calls=%fused_computation.4 | convolution fusion | flops 8920313856 | bytes 41446656 | tf_op jit(solution)/shard_map/dot_general | solution.py:98
  87.6 58.6 %reshape.251 = f32[117,4,4,18,258]{4,2,1,0,3:T(4,128)} reshape(f32[1872,18,258]{2,0,1:T(8,128)} %fusion) | data formatting | bytes 69548544 | tf_op jit(solution)/shard_map/reshape | solution.py:101
  146.2 72.5 %fusion.36 = (f32[117,1,1,16,256]{4,2,1,0,3:T(1,128)}, f32[117,1,1,16,256]{4,2,1,0,3:T(1,128)}, f32[117,1,1,16,256]{4,2,1,0,3:T(1,128)}, f32[117,1,1,16,256]{4,2...) fusion(f32[117,4,4,18,258]{4,2,1,0,3:T(4,128)} %reshape.251), kind=kLoop, calls=%fused_computation.92 | loop fusion | bytes 61341696 | tf_op jit(solution)/shard_map/slice | solution.py:126
  218.7 3.0 fusion.34
  222.1 1.8 scatter_custom_fusion
  224.5 4.7 copy.306
  229.2 6.1 copy.305
  235.3 6.1 copy.303
  241.4 6.1 copy.304
  247.5 6.1 copy.302
  253.6 6.1 copy.301
  259.7 6.1 copy.299
  265.8 6.1 copy.300
  271.9 7.4 fusion.6
  279.3 4.6 copy.310
  283.9 6.1 copy.309
  289.9 6.1 copy.307
  296.0 6.1 copy.308
  305.6 2.9 pad_maximum_fusion.5
  308.5 1.7 copy.227
  312.3 4.7 add_bitcast_fusion.1
  317.0 6.2 copy.314
  323.2 3.6 copy.313
  326.8 6.2 copy.311
  333.0 3.7 copy.312
  337.8 7.6 %pad_maximum_fusion = bf16[117,34,514]{2,0,1:T(8,128)(2,1)} fusion(bf16[117,34,1]{2,0,1:T(8,128)(2,1)S(1)} %copy.229, bf16[117,1,512]{2,0,1:T(8,128)(2,1)S(1)} %fusion.32, bf16[117,32,512]{2,0,1:T(8,128)(2,1)} %copy-done.3, bf16[117,1,512]{2,0,1:T(8,128)(2,1)S(1)} %broadcast_select_fusion, bf16[117,34,1]{2,0,1:T(8,128)(2,1)S(1)} %copy.228), kind=kLoop, calls=%fused_computation.2 | loop fusion | flops 20446920 | bytes 8178768 | tf_op jit(solution)/shard_map/concatenate | solution.py:23
  345.4 42.5 %slice.271 = bf16[117,17,257]{2,0,1:T(8,128)(2,1)S(1)} slice(bf16[117,34,514]{2,0,1:T(8,128)(2,1)} %pad_maximum_fusion), slice={[0:117:1], [0:34:2], [0:514:2]} | slice | bytes 2044692 | tf_op jit(solution)/shard_map/slice | solution.py:65
  388.0 42.9 %slice.273 = bf16[117,17,257]{2,0,1:T(8,128)(2,1)S(1)} slice(bf16[117,34,514]{2,0,1:T(8,128)(2,1)} %pad_maximum_fusion), slice={[0:117:1], [0:34:2], [1:514:2]} | slice | bytes 2044692 | tf_op jit(solution)/shard_map/slice | solution.py:65
  430.9 3.8 convolution_bitcast_fusion.15
  436.9 1.5 convolution_bitcast_fusion.12
  438.4 41.6 %slice.277 = bf16[117,17,257]{2,0,1:T(8,128)(2,1)} slice(bf16[117,34,514]{2,0,1:T(8,128)(2,1)} %pad_maximum_fusion), slice={[0:117:1], [1:34:2], [0:514:2]} | slice | bytes 2044692 | tf_op jit(solution)/shard_map/slice | solution.py:65
  480.0 43.0 %slice.279 = bf16[117,17,257]{2,0,1:T(8,128)(2,1)S(1)} slice(bf16[117,34,514]{2,0,1:T(8,128)(2,1)} %pad_maximum_fusion), slice={[0:117:1], [1:34:2], [1:514:2]} | slice | bytes 2044692 | tf_op jit(solution)/shard_map/slice | solution.py:65
  523.0 3.4 convolution_bitcast_fusion.11
  526.7 2.2 convolution_bitcast_fusion.9
  542.1 28.3 %stack.103 = f32[512,117,16]{0,2,1:T(8,128)} concatenate(f32[512,117,1]{0,2,1:T(1,128)S(1)} %stack.87, f32[512,117,1]{0,2,1:T(1,128)S(1)} %stack.88, f32[512,117,1]{0,2,1:T(1,128)S(1)} %stack.89, f32[512,117,1]{0,2,1:T(1,128)S(1)} %stack.90, f32[512,117,1]{0,2,1:T(1,128)S(1)} %stack.91, f32[512,117,1]{0,2,1:T(1,128)S(1)} %stack.92, f32[512,117,1]{0,2,1:T(1,128)S(1)} %stack.93, ...), dimensions={2} | concatenate | bytes 7667712 | tf_op jit(solution)/shard_map/stack | solution.py:87
  570.4 4.8 broadcast_multiply_fusion
  575.3 2.3 collective-permute-start.5
  577.6 4.7 add_bitcast_fusion
  583.0 4.6 collective-permute-done.6
  587.9 1.6 fusion.29
  589.4 1.6 fusion.28
  591.0 2.8 fusion.10
  595.7 2.5 slice_maximum_fusion
  598.2 8.6 %copy.220 = bf16[21,16,2,256,2]{0,4,3,2,1:T(2,128)(2,1)} copy(bf16[21,16,2,256,2]{0,3,1,4,2:T(8,128)(2,1)} %slice_maximum_fusion) | data formatting | bytes 1376256 | tf_op jit(solution)/shard_map/slice | solution.py:141
  606.8 4.9 copy.246
  611.7 5.0 pad_maximum_fusion.2
  616.7 8.6 %copy.221 = bf16[96,16,2,256,2]{0,4,3,2,1:T(2,128)(2,1)} copy(bf16[96,16,2,256,2]{0,3,1,4,2:T(8,128)(2,1)} %pad_maximum_fusion.2) | data formatting | bytes 6291456 | tf_op jit(solution)/shard_map/slice | solution.py:142
  625.3 7.4 copy.247
  632.7 98.3 %all-reduce.2.cloned.1.call-done = f32[512,1872]{0,1:T(8,128)} async-done(((f32[512,1872]{0,1:T(8,128)}), f32[512,1872]{0,1:T(8,128)}) %all-reduce.2.cloned.1.call-update) | async-done | bytes 3833872 | tf_op jit(solution)/shard_map/psum | solution.py:86
  (126 shorter events, 39.0 us)
Async XLA Ops:
  7.2 12.7 %copy-start.21 = (s32[32,512]{1,0:T(8,128)S(1)}, s32[32,512]{1,0:T(8,128)}, u32[]{:S(2)}) copy-start(s32[32,512]{1,0:T(8,128)} %param.13) | copy-start | bytes 196612
  7.2 723.8 %all-reduce.2.cloned.1.call-start = ((), (), s32[]{:S(2)}) async-start(), calls=%async_computation | async-start | bytes 7667712 | tf_op jit(solution)/shard_map/psum | solution.py:86
  7.2 12.7 %copy-start.13 = (bf16[1,96,32,512]{3,2,1,0:T(8,128)(2,1)S(1)}, bf16[1,96,32,512]{3,2,1,0:T(8,128)(2,1)}, u32[]{:S(2)}) copy-start(bf16[1,96,32,512]{3,2,1,0:T(8,128)(2,1)} %param.12) | copy-start | bytes 9437188
  16.8 28.8 %collective-permute-start.1 = (bf16[512,1,256]{0,2,1:T(8,128)(2,1)}, bf16[512,1,256]{0,2,1:T(8,128)(2,1)S(1)}, u32[]{:S(2)}, u32[]{:S(2)}) collective-permute-start(bf16[512,1,256]{0,2,1:T(8,128)(2,1)} %get-tuple-element.69), channel_id=1, source_target_pairs={{2,0},{4,2},{6,4},{8,6},{10,8},{12,10},{14,12},{0,14},{3,1},{5,3},... | collective-permute-start | bytes 786440 | tf_op jit(solution)/shard_map/ppermute | solution.py:27
  18.3 27.4 %collective-permute-start = (bf16[512,1,256]{0,2,1:T(8,128)(2,1)}, bf16[512,1,256]{0,2,1:T(8,128)(2,1)}, u32[]{:S(2)}, u32[]{:S(2)}) collective-permute-start(bf16[512,1,256]{0,2,1:T(8,128)(2,1)} %get-tuple-element.68), channel_id=1, source_target_pairs={{0,2},{2,4},{4,6},{6,8},{8,10},{10,12},{12,14},{14,0},{1,3},{3,5},... | collective-permute-start | bytes 786440 | tf_op jit(solution)/shard_map/ppermute | solution.py:25
  19.9 1.8 copy-start.18
  22.1 8.1 %copy-start.22 = (s32[512]{0:T(512)S(1)}, s32[512]{0:T(512)}, u32[]{:S(2)}) copy-start(s32[512]{0:T(512)} %param.14) | copy-start | bytes 6148
  22.1 11.8 %copy-start.14 = (bf16[512,1536]{1,0:T(8,128)(2,1)S(1)}, bf16[512,1536]{1,0:T(8,128)(2,1)}, u32[]{:S(2)}) copy-start(bf16[512,1536]{1,0:T(8,128)(2,1)} %param.17) | copy-start | bytes 4718596
  24.3 1.9 copy-start.3
  26.9 277.8 %collective-permute-start.11 = (bf16[117,1,512]{2,0,1:T(8,128)(2,1)}, bf16[117,1,512]{2,0,1:T(8,128)(2,1)}, u32[]{:S(2)}, u32[]{:S(2)}) collective-permute-start(bf16[117,1,512]{2,0,1:T(8,128)(2,1)} %get-tuple-element.74), channel_id=1, source_target_pairs={{2,0},{4,2},{6,4},{8,6},{10,8},{12,10},{14,12},{0,14},{3,1},{5,3},... | collective-permute-start | bytes 359432 | tf_op jit(solution)/shard_map/ppermute | solution.py:27
  28.8 14.2 %collective-permute-start.8 = (bf16[117,512]{1,0:T(8,128)(2,1)S(1)}, bf16[117,512]{1,0:T(8,128)(2,1)S(1)}, u32[]{:S(2)}, u32[]{:S(2)}) collective-permute-start(bf16[117,512]{1,0:T(8,128)(2,1)S(1)} %get-tuple-element.73), channel_id=1, source_target_pairs={{0,16},{16,0},{32,48},{48,32},{64,80},{80,64},{96,112},{112,96},{1... | collective-permute-start | bytes 359432 | tf_op jit(solution)/shard_map/ppermute | solution.py:15
  30.1 19.4 %collective-permute-start.7 = (bf16[117,1,512]{2,0,1:T(8,128)(2,1)S(1)}, bf16[117,1,512]{2,0,1:T(8,128)(2,1)S(1)}, u32[]{:S(2)}, u32[]{:S(2)}) collective-permute-start(bf16[117,1,512]{2,0,1:T(8,128)(2,1)S(1)} %get-tuple-element.72), channel_id=1, source_target_pairs={{0,2},{2,4},{4,6},{6,8},{8,10},{10,12},{12,14},{14,0},{1,3},{3,5},... | collective-permute-start | bytes 359432 | tf_op jit(solution)/shard_map/ppermute | solution.py:25
  43.0 12.9 %copy-start.2 = (bf16[1,512,16,256]{1,3,2,0:T(8,128)(2,1)S(1)}, bf16[1,512,16,256]{1,3,2,0:T(8,128)(2,1)}, u32[]{:S(2)}) copy-start(bf16[1,512,16,256]{1,3,2,0:T(8,128)(2,1)} %copy.200) | copy-start | bytes 12582916
  43.0 6.5 collective-permute-start.9
  46.7 4.7 collective-permute-start.3
  49.5 6.4 collective-permute-start.2
  49.5 252.6 %collective-permute-start.10 = (bf16[117,512]{1,0:T(8,128)(2,1)}, bf16[117,512]{1,0:T(8,128)(2,1)}, u32[]{:S(2)}, u32[]{:S(2)}) collective-permute-start(bf16[117,512]{1,0:T(8,128)(2,1)} %collective-permute-done.9), channel_id=1, source_target_pairs={{0,64},{64,0},{16,80},{80,16},{32,96},{96,32},{48,112},{112,48},{1... | collective-permute-start | bytes 359432 | tf_op jit(solution)/shard_map/ppermute | solution.py:15
  224.5 350.8 %collective-permute-start.4 = (bf16[117,512]{0,1:T(8,128)(2,1)}, bf16[117,512]{0,1:T(8,128)(2,1)}, u32[]{:S(2)}, u32[]{:S(2)}) collective-permute-start(bf16[117,512]{0,1:T(8,128)(2,1)} %convert_element_type.45), channel_id=1, source_target_pairs={{0,16},{16,0},{32,48},{48,32},{64,80},{80,64},{96,112},{112,96},{1... | collective-permute-start | bytes 359432 | tf_op jit(solution)/shard_map/ppermute | solution.py:15
  310.2 26.5 %collective-permute-start.13 = (bf16[117,34,1]{0,1,2:T(8,128)(2,1)S(1)}, bf16[117,34,1]{0,1,2:T(8,128)(2,1)S(1)}, u32[]{:S(2)}, u32[]{:S(2)}) collective-permute-start(bf16[117,34,1]{0,1,2:T(8,128)(2,1)S(1)} %copy.227), channel_id=1, source_target_pairs={{16,0},{32,16},{48,32},{64,48},{80,64},{96,80},{112,96},{0,112},{1... | collective-permute-start | bytes 23876 | tf_op jit(solution)/shard_map/ppermute | solution.py:27
  311.2 26.1 %collective-permute-start.12 = (bf16[117,34,1]{0,1,2:T(8,128)(2,1)S(1)}, bf16[117,34,1]{0,1,2:T(8,128)(2,1)S(1)}, u32[]{:S(2)}, u32[]{:S(2)}) collective-permute-start(bf16[117,34,1]{0,1,2:T(8,128)(2,1)S(1)} %copy.226), channel_id=1, source_target_pairs={{0,16},{16,32},{32,48},{48,64},{64,80},{80,96},{96,112},{112,0},{1... | collective-permute-start | bytes 23876 | tf_op jit(solution)/shard_map/ppermute | solution.py:25
  317.0 6.2 copy-start.10
  326.8 6.2 copy-start.9
  388.0 46.7 %copy-start.4 = (bf16[117,17,257]{2,0,1:T(8,128)(2,1)}, bf16[117,17,257]{2,0,1:T(8,128)(2,1)S(1)}, u32[]{:S(2)}) copy-start(bf16[117,17,257]{2,0,1:T(8,128)(2,1)S(1)} %slice.271) | copy-start | bytes 3067042
  430.9 3.8 copy-start
  523.0 3.7 copy-start.1
  529.7 1.4 copy-start.5
  533.3 1.4 copy-start.6
  537.0 0.9 copy-start.16
  537.0 1.1 copy-start.17
  537.0 1.5 copy-start.15
  575.2 2.3 copy-start.8
  575.3 7.3 copy-start.11
  575.3 7.3 copy-start.12
  575.3 7.0 collective-permute-start.5
  582.3 5.3 collective-permute-start.6
  582.5 8.5 %copy-start.19 = (f32[16,256]{1,0:T(8,128)S(1)}, f32[16,256]{1,0:T(8,128)}, u32[]{:S(2)}) copy-start(f32[16,256]{1,0:T(8,128)} %slice.257) | copy-start | bytes 49156
  582.5 8.5 %copy-start.20 = (f32[16,256]{1,0:T(8,128)S(1)}, f32[16,256]{1,0:T(8,128)}, u32[]{:S(2)}) copy-start(f32[16,256]{1,0:T(8,128)} %slice.264) | copy-start | bytes 49156
  594.3 1.3 copy-start.7
Sparse Core Ops, SparseCore 0:
  575.4 155.5 all-reduce.1
where the time goes:
time: 754 us; the launch traced here: 742 us
  local copies, waits for them, and re-layouts  495 us (66%)
  waiting for transfers between devices  107 us (14%)
  other arithmetic  63.1 us (8%)
  matrix products  43.5 us (6%)
  starting transfers between devices  17.7 us (2%)
  between operations  14.9 us (2%)
    slice x4, local copies, waits for them, and re-layouts, on_device(): padded[:, row_par::2, col_par::2]  170 us
    unnamed x70, local copies, waits for them, and re-layouts  120 us
    psum x1, waiting for transfers between devices, on_device(): lax.psum(jnp.stack(terms, axis=-1).reshape(grad_tokens.shape[0], channels...  98.3 us
    slice x1, local copies, waits for them, and re-layouts, on_device(): spread_all[:, row_off, col_off, row_start:row_start + tok_rows, col_start...  72.5 us
    reshape x1, local copies, waits for them, and re-layouts, on_device(): spread_all = spread_all.reshape(channels, 4, 4, tok_rows + 2, tok_cols + 2)  58.6 us
    another operation x17, local copies, waits for them, and re-layouts, on_device(): jnp.stack(terms, axis=-1).reshape(grad_tokens.shape[0], channels * 16)  32.4 us
    dot_general x1, matrix products, on_device(): lax.dot_general(weights, grad_ext, (((0,), (0,)), ((), ())), preferred_el...  22.9 us
    dot_general x16, matrix products, on_device(): lax.dot_general(grad_tokens, window, (((1, 2), (1, 2)), ((), ())), prefer...  20.6 us
  transfers between devices with their start and end apart: 15, of which 3 were waited for; matrix products, arithmetic and copies ran while one was open for 79% of the time, Pallas kernels for 0%

commit v1 on v0

--- a/solution.py
+++ b/solution.py
@@ -84,8 +84,10 @@
         for window in windows
     ]
     summed = lax.psum(
-        jnp.stack(terms, axis=-1).reshape(grad_tokens.shape[0], channels * 16) * scale,
-        ("lon", "lat", "batch"),
+        lax.psum(
+            jnp.stack(terms, axis=-1).reshape(grad_tokens.shape[0], channels * 16) * scale, "lon"
+        ),
+        ("lat", "batch"),
     )
     kernel_own = lax.dynamic_slice_in_dim(
         summed, lax.axis_index(("lat", "batch")) * share, share, 0

time: 754 us -> 709 us (0.940)
  waiting for transfers between devices: 107 us -> 59.8 us
    psum x1, waiting for transfers between devices: 98.3 us -> 33.5 us  [on_device(): lax.psum(jnp.stack(terms, axis=-1).reshape(grad_tokens.shape[0], channels...]
    psum x0 -> x1, waiting for transfers between devices: none -> 15.7 us  [on_device(): lax.psum(lax.psum(jnp.stack(terms, axis=-1).reshape(grad_tokens.shape[0],...]
  transfers between devices with their start and end apart: 15 -> 16, of which waited for: 3 -> 4; matrix products, arithmetic and copies ran while one was open for 79% -> 49% of each run, Pallas kernels for 0% -> 0%
where the time goes in v1:
time: 709 us; the launch traced here: 697 us
  local copies, waits for them, and re-layouts  500 us (71%)
  waiting for transfers between devices  59.8 us (8%)
  other arithmetic  57.5 us (8%)
  matrix products  44.2 us (6%)
  starting transfers between devices  20.1 us (3%)
  between operations  14.9 us (2%)
    slice x4, local copies, waits for them, and re-layouts, on_device(): padded[:, row_par::2, col_par::2]  170 us
    unnamed x70, local copies, waits for them, and re-layouts  126 us
    slice x1, local copies, waits for them, and re-layouts, on_device(): spread_all[:, row_off, col_off, row_start:row_start + tok_rows, col_start...  72.7 us
    reshape x1, local copies, waits for them, and re-layouts, on_device(): spread_all = spread_all.reshape(channels, 4, 4, tok_rows + 2, tok_cols + 2)  58.6 us
    psum x1, waiting for transfers between devices, on_device(): lax.psum(jnp.stack(terms, axis=-1).reshape(grad_tokens.shape[0], channels...  33.5 us
    another operation x17, local copies, waits for them, and re-layouts, on_device(): jnp.stack(terms, axis=-1).reshape(grad_tokens.shape[0], channels * 16)  32.4 us
    dot_general x1, matrix products, on_device(): lax.dot_general(weights, grad_ext, (((0,), (0,)), ((), ())), preferred_el...  23.6 us
    dot_general x16, matrix products, on_device(): lax.dot_general(grad_tokens, window, (((1, 2), (1, 2)), ((), ())), prefer...  20.6 us
  transfers between devices with their start and end apart: 16, of which 4 were waited for; matrix products, arithmetic and copies ran while one was open for 49% of the time, Pallas kernels for 0%

profile of v1, /device:TPU:1, one launch (start us, length us, event | category | flops | bytes accessed | tf_op | source)
XLA Modules:
  0.0 696.8 jit_solution(5908889463700152482)
XLA Ops:
  7.2 7.8 %copy.200 = bf16[1,512,16,256]{1,3,2,0:T(8,128)(2,1)} copy(bf16[1,512,16,256]{3,2,1,0:T(8,128)(2,1)} %param.15) | data formatting | bytes 8388608 | tf_op args[4]
  15.0 1.9 fusion.37
  18.3 1.6 collective-permute-start
  19.9 1.8 copy.317
  22.1 2.2 maximum_multiply_fusion
  24.3 1.9 copy-done.3
  26.2 2.0 collective-permute-start.11
  33.3 1.6 copy.199
  34.8 7.6 %copy.251 = bf16[512,16,256]{0,2,1:T(8,128)(2,1)} copy(bf16[512,16,256]{2,1,0:T(8,128)(2,1)} %bitcast.187) | data formatting | bytes 8388608 | tf_op jit(solution)/shard_map/squeeze | solution.py:95
  42.4 2.6 collective-permute-start.9
  46.1 2.8 collective-permute-start.3
  48.9 2.0 collective-permute-start.10
  50.9 4.4 collective-permute-done.2
  55.3 6.6 pad_maximum_fusion.1
  61.9 2.3 slice.297
  67.0 1.9 pad_maximum_fusion.5
  71.5 23.6 %fusion = f32[1872,18,258]{2,0,1:T(8,128)} fusion(bf16[512,1,258]{0,2,1:T(8,128)(2,1)S(1)} %get-tuple-element.65, bf16[512,16,258]{0,2,1:T(8,128)(2,1)} %slice.297, bf16[512,1,258]{0,2,1:T(8,128)(2,1)S(1)} %get-tuple-element.64, bf16[512,1536]{0,1:T(8,128)(2,1)} %copy.199, bf16[512,336]{0,1:T(8,128)(2,1)S(1)} %copy-done.22), kind=kOutput, calls=%fused_computation.4 | convolution fusion | flops 8920313856 | bytes 41446656 | tf_op jit(solution)/shard_map/dot_general | solution.py:100
  95.2 58.6 %reshape.251 = f32[117,4,4,18,258]{4,2,1,0,3:T(4,128)} reshape(f32[1872,18,258]{2,0,1:T(8,128)} %fusion) | data formatting | bytes 69548544 | tf_op jit(solution)/shard_map/reshape | solution.py:103
  154.9 7.6 %pad_maximum_fusion = bf16[117,34,514]{2,0,1:T(8,128)(2,1)} fusion(bf16[117,34,1]{2,0,1:T(8,128)(2,1)S(1)} %copy.229, bf16[117,1,512]{2,0,1:T(8,128)(2,1)S(1)} %fusion.32, bf16[117,32,512]{2,0,1:T(8,128)(2,1)} %copy-done.3, bf16[117,1,512]{2,0,1:T(8,128)(2,1)S(1)} %broadcast_select_fusion, bf16[117,34,1]{2,0,1:T(8,128)(2,1)S(1)} %copy.228), kind=kLoop, calls=%fused_computation.2 | loop fusion | flops 20446920 | bytes 8178768 | tf_op jit(solution)/shard_map/concatenate | solution.py:23
  162.6 42.5 %slice.271 = bf16[117,17,257]{2,0,1:T(8,128)(2,1)S(1)} slice(bf16[117,34,514]{2,0,1:T(8,128)(2,1)} %pad_maximum_fusion), slice={[0:117:1], [0:34:2], [0:514:2]} | slice | bytes 2044692 | tf_op jit(solution)/shard_map/slice | solution.py:65
  205.1 42.9 %slice.273 = bf16[117,17,257]{2,0,1:T(8,128)(2,1)S(1)} slice(bf16[117,34,514]{2,0,1:T(8,128)(2,1)} %pad_maximum_fusion), slice={[0:117:1], [0:34:2], [1:514:2]} | slice | bytes 2044692 | tf_op jit(solution)/shard_map/slice | solution.py:65
  248.1 3.8 convolution_bitcast_fusion.15
  255.5 41.6 %slice.277 = bf16[117,17,257]{2,0,1:T(8,128)(2,1)} slice(bf16[117,34,514]{2,0,1:T(8,128)(2,1)} %pad_maximum_fusion), slice={[0:117:1], [1:34:2], [0:514:2]} | slice | bytes 2044692 | tf_op jit(solution)/shard_map/slice | solution.py:65
  297.1 43.0 %slice.279 = bf16[117,17,257]{2,0,1:T(8,128)(2,1)S(1)} slice(bf16[117,34,514]{2,0,1:T(8,128)(2,1)} %pad_maximum_fusion), slice={[0:117:1], [1:34:2], [1:514:2]} | slice | bytes 2044692 | tf_op jit(solution)/shard_map/slice | solution.py:65
  340.1 3.4 convolution_bitcast_fusion.11
  343.8 2.2 convolution_bitcast_fusion.9
  359.2 28.3 %stack.103 = f32[512,117,16]{0,2,1:T(8,128)} concatenate(f32[512,117,1]{0,2,1:T(1,128)S(1)} %stack.87, f32[512,117,1]{0,2,1:T(1,128)S(1)} %stack.88, f32[512,117,1]{0,2,1:T(1,128)S(1)} %stack.89, f32[512,117,1]{0,2,1:T(1,128)S(1)} %stack.90, f32[512,117,1]{0,2,1:T(1,128)S(1)} %stack.91, f32[512,117,1]{0,2,1:T(1,128)S(1)} %stack.92, f32[512,117,1]{0,2,1:T(1,128)S(1)} %stack.93, ...), dimensions={2} | concatenate | bytes 7667712 | tf_op jit(solution)/shard_map/stack | solution.py:88
  387.5 4.8 broadcast_multiply_fusion
  392.4 72.7 %fusion.36 = (f32[117,1,1,16,256]{4,2,1,0,3:T(1,128)}, f32[117,1,1,16,256]{4,2,1,0,3:T(1,128)}, f32[117,1,1,16,256]{4,2,1,0,3:T(1,128)}, f32[117,1,1,16,256]{4,2...) fusion(f32[117,4,4,18,258]{4,2,1,0,3:T(4,128)} %reshape.251), kind=kLoop, calls=%fused_computation.92 | loop fusion | bytes 61341696 | tf_op jit(solution)/shard_map/slice | solution.py:128
  465.1 33.5 %all-reduce.3.cloned.1.call-done = f32[512,1872]{0,1:T(8,128)} async-done(((f32[512,1872]{0,1:T(8,128)}), f32[512,1872]{0,1:T(8,128)}) %all-reduce.3.cloned.1.call-update) | async-done | bytes 3833872 | tf_op jit(solution)/shard_map/psum | solution.py:87
  498.6 3.0 fusion.34
  501.5 4.6 copy.310
  506.1 6.1 copy.309
  512.2 6.1 copy.307
  518.3 6.1 copy.308
  524.9 1.8 scatter_custom_fusion
  526.7 6.5 copy.306
  533.3 6.1 copy.305
  539.4 6.1 copy.303
  545.5 6.1 copy.304
  551.6 6.1 copy.302
  557.7 6.1 copy.301
  563.8 6.1 copy.299
  569.9 6.1 copy.300
  576.0 7.8 %fusion.6 = (bf16[117,16,256,1]{0,2,1,3:T(8,128)(2,1)S(1)}, bf16[117,16,256,1]{0,2,1,3:T(8,128)(2,1)}) fusion(f32[117,1,1,16,256]{0,4,3,2,1:T(8,128)} %copy.306, f32[117,1,1,16,256]{0,4,3,2,1:T(8,128)} %copy.305, f32[117,1,1,16,256]{0,4,3,2,1:T(8,128)} %copy.303, f32[117,1,1,16,256]{0,4,3,2,1:T(8,128)} %copy.304, f32[16,256]{1,0:T(8,128)S(1)} %slice.246, ...), kind=kLoop, calls=%fused_computation.17 | loop fusion | flops 4792320 | bytes 17285120 | tf_op jit(solution)/shard_map/convert_element_type | solution.py:139
  584.1 2.0 add_bitcast_fusion.1
  586.1 4.6 copy.314
  590.7 6.1 copy.313
  596.8 6.1 copy.311
  602.9 6.1 copy.312
  609.0 2.3 collective-permute-start.5
  611.4 4.8 add_bitcast_fusion
  616.1 2.3 collective-permute-start.6
  618.9 6.2 collective-permute-done.6
  625.4 1.6 fusion.29
  626.9 1.6 fusion.28
  628.5 2.8 fusion.10
  633.2 2.5 slice_maximum_fusion
  635.6 8.6 %copy.220 = bf16[21,16,2,256,2]{0,4,3,2,1:T(2,128)(2,1)} copy(bf16[21,16,2,256,2]{0,3,1,4,2:T(8,128)(2,1)} %slice_maximum_fusion) | data formatting | bytes 1376256 | tf_op jit(solution)/shard_map/slice | solution.py:143
  644.2 4.9 copy.246
  649.1 5.0 pad_maximum_fusion.2
  654.1 8.6 %copy.221 = bf16[96,16,2,256,2]{0,4,3,2,1:T(2,128)(2,1)} copy(bf16[96,16,2,256,2]{0,3,1,4,2:T(8,128)(2,1)} %pad_maximum_fusion.2) | data formatting | bytes 6291456 | tf_op jit(solution)/shard_map/slice | solution.py:144
  662.7 7.4 %copy.247 = bf16[1,96,32,512]{3,2,1,0:T(8,128)(2,1)} copy(bf16[1,96,32,512]{1,3,2,0:T(8,128)(2,1)} %bitcast.186) | data formatting | bytes 6291456
  670.1 15.7 %all-reduce.5.cloned.1.call-done = f32[512,1872]{0,1:T(8,128)} async-done(((f32[512,1872]{0,1:T(8,128)}), f32[512,1872]{0,1:T(8,128)}) %all-reduce.5.cloned.1.call-update) | async-done | bytes 3833872 | tf_op jit(solution)/shard_map/psum | solution.py:86
  (129 shorter events, 38.9 us)
Async XLA Ops:
  7.2 12.7 %copy-start.20 = (s32[32,512]{1,0:T(8,128)S(1)}, s32[32,512]{1,0:T(8,128)}, u32[]{:S(2)}) copy-start(s32[32,512]{1,0:T(8,128)} %param.13) | copy-start | bytes 196612
  7.2 491.4 %all-reduce.3.cloned.1.call-start = ((), (), s32[]{:S(2)}) async-start(), calls=%async_computation | async-start | bytes 7667712 | tf_op jit(solution)/shard_map/psum | solution.py:87
  7.2 12.7 %copy-start.12 = (bf16[1,96,32,512]{3,2,1,0:T(8,128)(2,1)S(1)}, bf16[1,96,32,512]{3,2,1,0:T(8,128)(2,1)}, u32[]{:S(2)}) copy-start(bf16[1,96,32,512]{3,2,1,0:T(8,128)(2,1)} %param.12) | copy-start | bytes 9437188
  16.8 28.2 %collective-permute-start.1 = (bf16[512,1,256]{0,2,1:T(8,128)(2,1)}, bf16[512,1,256]{0,2,1:T(8,128)(2,1)S(1)}, u32[]{:S(2)}, u32[]{:S(2)}) collective-permute-start(bf16[512,1,256]{0,2,1:T(8,128)(2,1)} %get-tuple-element.69), channel_id=1, source_target_pairs={{2,0},{4,2},{6,4},{8,6},{10,8},{12,10},{14,12},{0,14},{3,1},{5,3},... | collective-permute-start | bytes 786440 | tf_op jit(solution)/shard_map/ppermute | solution.py:27
  18.3 26.8 %collective-permute-start = (bf16[512,1,256]{0,2,1:T(8,128)(2,1)}, bf16[512,1,256]{0,2,1:T(8,128)(2,1)}, u32[]{:S(2)}, u32[]{:S(2)}) collective-permute-start(bf16[512,1,256]{0,2,1:T(8,128)(2,1)} %get-tuple-element.68), channel_id=1, source_target_pairs={{0,2},{2,4},{4,6},{6,8},{8,10},{10,12},{12,14},{14,0},{1,3},{3,5},... | collective-permute-start | bytes 786440 | tf_op jit(solution)/shard_map/ppermute | solution.py:25
  19.9 1.8 copy-start.17
  22.1 7.5 %copy-start.21 = (s32[512]{0:T(512)S(1)}, s32[512]{0:T(512)}, u32[]{:S(2)}) copy-start(s32[512]{0:T(512)} %param.14) | copy-start | bytes 6148
  22.1 11.2 %copy-start.13 = (bf16[512,1536]{1,0:T(8,128)(2,1)S(1)}, bf16[512,1536]{1,0:T(8,128)(2,1)}, u32[]{:S(2)}) copy-start(bf16[512,1536]{1,0:T(8,128)(2,1)} %param.17) | copy-start | bytes 4718596
  24.3 1.9 copy-start.3
  26.2 40.8 %collective-permute-start.11 = (bf16[117,1,512]{2,0,1:T(8,128)(2,1)S(1)}, bf16[117,1,512]{2,0,1:T(8,128)(2,1)S(1)}, u32[]{:S(2)}, u32[]{:S(2)}) collective-permute-start(bf16[117,1,512]{2,0,1:T(8,128)(2,1)S(1)} %get-tuple-element.74), channel_id=1, source_target_pairs={{2,0},{4,2},{6,4},{8,6},{10,8},{12,10},{14,12},{0,14},{3,1},{5,3},... | collective-permute-start | bytes 359432 | tf_op jit(solution)/shard_map/ppermute | solution.py:27
  28.2 14.2 %collective-permute-start.8 = (bf16[117,512]{1,0:T(8,128)(2,1)S(1)}, bf16[117,512]{1,0:T(8,128)(2,1)S(1)}, u32[]{:S(2)}, u32[]{:S(2)}) collective-permute-start(bf16[117,512]{1,0:T(8,128)(2,1)S(1)} %get-tuple-element.73), channel_id=1, source_target_pairs={{0,16},{16,0},{32,48},{48,32},{64,80},{80,64},{96,112},{112,96},{1... | collective-permute-start | bytes 359432 | tf_op jit(solution)/shard_map/ppermute | solution.py:15
  29.5 19.4 %collective-permute-start.7 = (bf16[117,1,512]{2,0,1:T(8,128)(2,1)S(1)}, bf16[117,1,512]{2,0,1:T(8,128)(2,1)S(1)}, u32[]{:S(2)}, u32[]{:S(2)}) collective-permute-start(bf16[117,1,512]{2,0,1:T(8,128)(2,1)S(1)} %get-tuple-element.72), channel_id=1, source_target_pairs={{0,2},{2,4},{4,6},{6,8},{8,10},{10,12},{12,14},{14,0},{1,3},{3,5},... | collective-permute-start | bytes 359432 | tf_op jit(solution)/shard_map/ppermute | solution.py:25
  42.4 12.9 %copy-start.2 = (bf16[1,512,16,256]{1,3,2,0:T(8,128)(2,1)S(1)}, bf16[1,512,16,256]{1,3,2,0:T(8,128)(2,1)}, u32[]{:S(2)}) copy-start(bf16[1,512,16,256]{1,3,2,0:T(8,128)(2,1)} %copy.200) | copy-start | bytes 12582916
  42.4 6.5 collective-permute-start.9
  46.1 4.9 collective-permute-start.3
  48.9 6.4 collective-permute-start.2
  48.9 16.4 %collective-permute-start.10 = (bf16[117,512]{1,0:T(8,128)(2,1)S(1)}, bf16[117,512]{1,0:T(8,128)(2,1)S(1)}, u32[]{:S(2)}, u32[]{:S(2)}) collective-permute-start(bf16[117,512]{1,0:T(8,128)(2,1)S(1)} %collective-permute-done.9), channel_id=1, source_target_pairs={{0,64},{64,0},{16,80},{80,16},{32,96},{96,32},{48,112},{112,48},{1... | collective-permute-start | bytes 359432 | tf_op jit(solution)/shard_map/ppermute | solution.py:15
  68.9 2.6 copy-start.22
  69.4 84.4 %collective-permute-start.13 = (bf16[117,34,1]{0,1,2:T(8,128)(2,1)S(1)}, bf16[117,34,1]{0,1,2:T(8,128)(2,1)S(1)}, u32[]{:S(2)}, u32[]{:S(2)}) collective-permute-start(bf16[117,34,1]{0,1,2:T(8,128)(2,1)S(1)} %copy.227), channel_id=1, source_target_pairs={{16,0},{32,16},{48,32},{64,48},{80,64},{96,80},{112,96},{0,112},{1... | collective-permute-start | bytes 23876 | tf_op jit(solution)/shard_map/ppermute | solution.py:27
  70.4 84.0 %collective-permute-start.12 = (bf16[117,34,1]{0,1,2:T(8,128)(2,1)S(1)}, bf16[117,34,1]{0,1,2:T(8,128)(2,1)S(1)}, u32[]{:S(2)}, u32[]{:S(2)}) collective-permute-start(bf16[117,34,1]{0,1,2:T(8,128)(2,1)S(1)} %copy.226), channel_id=1, source_target_pairs={{0,16},{16,32},{32,48},{48,64},{64,80},{80,96},{96,112},{112,0},{1... | collective-permute-start | bytes 23876 | tf_op jit(solution)/shard_map/ppermute | solution.py:25
  205.1 46.7 %copy-start.4 = (bf16[117,17,257]{2,0,1:T(8,128)(2,1)}, bf16[117,17,257]{2,0,1:T(8,128)(2,1)S(1)}, u32[]{:S(2)}) copy-start(bf16[117,17,257]{2,0,1:T(8,128)(2,1)S(1)} %slice.271) | copy-start | bytes 3067042
  248.0 3.8 copy-start
  340.1 3.7 copy-start.1
  346.8 1.4 copy-start.5
  350.4 1.4 copy-start.6
  354.1 0.9 copy-start.15
  354.1 1.1 copy-start.16
  354.1 1.5 copy-start.14
  392.4 293.4 %all-reduce.5.cloned.1.call-start = ((), (), s32[]{:S(2)}) async-start(), calls=%async_computation.1 | async-start | bytes 7667712 | tf_op jit(solution)/shard_map/psum | solution.py:86
  526.7 82.4 %collective-permute-start.4 = (bf16[117,512]{0,1:T(8,128)(2,1)S(1)}, bf16[117,512]{0,1:T(8,128)(2,1)S(1)}, u32[]{:S(2)}, u32[]{:S(2)}) collective-permute-start(bf16[117,512]{0,1:T(8,128)(2,1)S(1)} %convert_element_type.45), channel_id=1, source_target_pairs={{0,16},{16,0},{32,48},{48,32},{64,80},{80,64},{96,112},{112,96},{1... | collective-permute-start | bytes 359432 | tf_op jit(solution)/shard_map/ppermute | solution.py:15
  576.0 7.8 %copy-start.8 = (f32[117,1,1,16,256]{0,4,3,2,1:T(8,128)S(1)}, f32[117,1,1,16,256]{0,4,3,2,1:T(8,128)}, u32[]{:S(2)}) copy-start(f32[117,1,1,16,256]{0,4,3,2,1:T(8,128)} %copy.309) | copy-start | bytes 5750788
  576.0 7.8 %copy-start.9 = (f32[117,1,1,16,256]{0,4,3,2,1:T(8,128)S(1)}, f32[117,1,1,16,256]{0,4,3,2,1:T(8,128)}, u32[]{:S(2)}) copy-start(f32[117,1,1,16,256]{0,4,3,2,1:T(8,128)} %copy.307) | copy-start | bytes 5750788
  576.0 8.1 %copy-start.10 = (f32[117,1,1,16,256]{0,4,3,2,1:T(8,128)S(1)}, f32[117,1,1,16,256]{0,4,3,2,1:T(8,128)}, u32[]{:S(2)}) copy-start(f32[117,1,1,16,256]{0,4,3,2,1:T(8,128)} %copy.308) | copy-start | bytes 5750788
  609.0 9.4 %copy-start.11 = (bf16[117,16,256,1]{0,2,1,3:T(8,128)(2,1)S(1)}, bf16[117,16,256,1]{0,2,1,3:T(8,128)(2,1)}, u32[]{:S(2)}) copy-start(bf16[117,16,256,1]{0,2,1,3:T(8,128)(2,1)} %get-tuple-element.80) | copy-start | bytes 2875396
  609.0 7.1 %collective-permute-start.5 = (bf16[117,512]{0,1:T(8,128)(2,1)S(1)}, bf16[117,512]{0,1:T(8,128)(2,1)S(1)}, u32[]{:S(2)}, u32[]{:S(2)}) collective-permute-start(bf16[117,512]{0,1:T(8,128)(2,1)S(1)} %collective-permute-done.4), channel_id=1, source_target_pairs={{0,32},{32,0},{16,48},{48,16},{64,96},{96,64},{80,112},{112,80},{1... | collective-permute-start | bytes 359432 | tf_op jit(solution)/shard_map/ppermute | solution.py:15
  616.1 9.0 %collective-permute-start.6 = (bf16[117,512]{0,1:T(8,128)(2,1)S(1)}, bf16[117,512]{0,1:T(8,128)(2,1)S(1)}, u32[]{:S(2)}, u32[]{:S(2)}) collective-permute-start(bf16[117,512]{0,1:T(8,128)(2,1)S(1)} %collective-permute-done.5), channel_id=1, source_target_pairs={{0,64},{64,0},{16,80},{80,16},{32,96},{96,32},{48,112},{112,48},{1... | collective-permute-start | bytes 359432 | tf_op jit(solution)/shard_map/ppermute | solution.py:15
  618.4 10.1 %copy-start.18 = (f32[16,256]{1,0:T(8,128)S(1)}, f32[16,256]{1,0:T(8,128)}, u32[]{:S(2)}) copy-start(f32[16,256]{1,0:T(8,128)} %slice.257) | copy-start | bytes 49156
  618.4 10.1 %copy-start.19 = (f32[16,256]{1,0:T(8,128)S(1)}, f32[16,256]{1,0:T(8,128)}, u32[]{:S(2)}) copy-start(f32[16,256]{1,0:T(8,128)} %slice.264) | copy-start | bytes 49156
  631.8 1.3 copy-start.7
Sparse Core Ops, SparseCore 0:
  392.5 106.0 all-reduce.2
  501.1 184.5 all-reduce.4
